TPU v7x, 32 devices: a whole 2x2x4 slice. The times are simulated.
32 devices in a mesh: mesh: 8 (over y, x, core), band: 4 (over z).
Axes of the slice: x: 2, y: 2, z: 4, core: 2. Of those that a mesh axis runs over, the one named last changes fastest.
Arguments:
- states: float32 [2, 64, 8192], P(None, 'band', 'mesh'), may hold values from -6 to 6
- frozen: float32 [2, 32, 8192], P(None, 'band', 'mesh'), may hold values from -0.125 to 0.125
- weights: float32 [8, 8192], P(None, 'mesh'), may hold values from 0.1 to 1
- potential: float32 [8192], P('mesh'), may hold values from -2 to 2
- send_list: int32 [8, 8, 256], P('mesh'), may hold values from 0 to 1023
- neighbours: int32 [8, 8192], P(None, 'mesh'), may hold values from 0 to 3071, as said below
Outputs:
- evolved: float32 [2, 64, 8192], P(None, 'band', 'mesh')
Inputs may be any that keep to these rules, and one draw needn't show every extreme that they name: `neighbours`: an entry below 1024 names a point of the same part; an entry 1024 + s * 256 + c names ghost slot c from part s, where part s is at most 3 parts away in the cyclic order of parts or exactly half the number of parts away, and every part names ghost slots from all those parts. Slots of send_list[s, i] that part i never names hold arbitrary points of part s.
All inputs are finite; a program needn't handle non-finite values.
Results may differ from a plain program's by a relative error of at most 0.0001.
Values sent between devices are 32-bit elements; how exact they have to be, the bound alone decides.
No kernel may reach another device: no remote copies, remote signals or barrier semaphores. Data moves between devices by JAX's collectives and lax.ppermute only.
A program may use at most 128 MiB of HBM per device.

v0:
```python
import jax
import jax.numpy as jnp
from jax import lax
from jax.sharding import PartitionSpec as P

NBRS = 8
TERMS = 4
time_step = 0.3


def rotate(field):
    return jnp.stack([field[1], -field[0]])


def body(states, frozen, weights, potential, send_list, neighbours):
    parts = lax.axis_size("mesh")
    rows = states.shape[1]
    capacity = send_list.shape[2]
    routes = send_list[0]
    full_frozen = lax.all_gather(frozen, "band", axis=1, tiled=True)
    total = states
    term = states
    for order in range(1, TERMS + 1):
        paired = jnp.stack([term, rotate(term)])
        partial_intersection = jnp.einsum(
            "cmp,ocjp->omj", full_frozen, paired, precision=lax.Precision.HIGHEST
        )
        intersection = lax.psum(partial_intersection, "mesh")
        packed = jnp.take(term, routes.reshape(-1), axis=2).reshape(2, rows, parts, capacity)
        arrived = lax.all_to_all(packed, "mesh", split_axis=2, concat_axis=2, tiled=True)
        extended = jnp.concatenate([term, arrived.reshape(2, rows, parts * capacity)], axis=2)
        stencil = jnp.zeros_like(term)
        for apply_order in range(NBRS):
            stencil = stencil + weights[apply_order] * (
                jnp.take(extended, neighbours[apply_order], axis=2) - term
            )
        blocks = jnp.stack(
            [
                jnp.stack([intersection[0], -intersection[1]]),
                jnp.stack([intersection[1], intersection[0]]),
            ]
        )
        exchange = jnp.einsum("dmp,cdmj->cjp", full_frozen, blocks, precision=lax.Precision.HIGHEST)
        image = -0.5 * stencil + potential * term - exchange
        term = time_step / order * rotate(image)
        total = total + term
    return total


def solution(mesh):
    return jax.shard_map(
        body,
        mesh=mesh,
        in_specs=(
            P(None, "band", "mesh"),
            P(None, "band", "mesh"),
            P(None, "mesh"),
            P("mesh"),
            P("mesh", None, None),
            P(None, "mesh"),
        ),
        out_specs=P(None, "band", "mesh"),
        check_vma=False,
    )
```

profile of v0, /device:TPU:0, one launch (start us, length us, event | category | flops | bytes accessed | tf_op | source)
XLA Modules:
  0.0 581.9 jit_solution(13586005560089532101)
XLA Ops:
  2.1 14.4 %gather_fusion = f32[2048,2,16]{2,1,0:T(2,128)} fusion(f32[2,16,1024]{1,0,2:T(2,128)S(1)} %copy.119, s32[2048]{0:T(1024)S(1)} %fusion.108), kind=kCustom, calls=%fused_computation.clone | custom fusion | bytes 532480 | tf_op jit(solution)/shard_map/jit(_take)/gather | solution.py:29
  16.5 10.0 %broadcast_select_fusion.3 = f32[2048,2,16]{2,1,0:T(2,128)S(1)} fusion(f32[2048,2,16]{2,1,0:T(2,128)} %gather_fusion, pred[2048]{0:T(1024)(128)(4,1)S(1)} %compare_and_fusion), kind=kLoop, calls=%fused_computation.39 | loop fusion | flops 65536 | bytes 526336 | tf_op jit(solution)/shard_map/jit(_take)/select_n | solution.py:29
  28.5 5.2 all-to-all-start
  39.6 14.2 %all_gather.3 = f32[2,32,1024]{2,1,0:T(8,128)S(1)} all-gather(f32[2,8,1024]{2,1,0:T(8,128)S(1)} %copy-done.34), channel_id=1, replica_groups=mesh['mesh'=8,'band'=4] {'band'}, dimensions={1}, use_global_device_ids=true | all-gather | bytes 327680 | tf_op jit(solution)/shard_map/all_gather | solution.py:20
  54.3 23.0 %psum.28 = f32[2,32,16]{1,2,0:T(8,128)S(1)} all-reduce(f32[2,32,16]{1,2,0:T(8,128)S(1)} %convolution_bitcast_fusion.7), channel_id=1, replica_groups=mesh['mesh'=8,'band'=4] {'mesh'}, use_global_device_ids=true, to_apply=%region_0.3 | all-reduce | flops 1024 | bytes 8192 | tf_op jit(solution)/shard_map/psum | solution.py:28
  79.9 4.1 copy.122
  84.0 7.6 %gather_fusion.1 = f32[1024,2,16]{2,1,0:T(2,128)} fusion(f32[2,16,3072]{1,0,2:T(2,128)S(1)} %copy.122, s32[1024]{0:T(1024)} %fusion.109), kind=kCustom, calls=%fused_computation.1.clone | custom fusion | bytes 266240 | tf_op jit(solution)/shard_map/jit(_take)/gather | solution.py:35
  93.7 7.6 %gather_fusion.2 = f32[1024,2,16]{2,1,0:T(2,128)} fusion(f32[2,16,3072]{1,0,2:T(2,128)S(1)} %copy.122, s32[1024]{0:T(1024)} %fusion.110), kind=kCustom, calls=%fused_computation.5.clone | custom fusion | bytes 266240 | tf_op jit(solution)/shard_map/jit(_take)/gather | solution.py:35
  103.3 7.6 %gather_fusion.3 = f32[1024,2,16]{2,1,0:T(2,128)} fusion(f32[2,16,3072]{1,0,2:T(2,128)S(1)} %copy.122, s32[1024]{0:T(1024)} %fusion.111), kind=kCustom, calls=%fused_computation.6.clone | custom fusion | bytes 266240 | tf_op jit(solution)/shard_map/jit(_take)/gather | solution.py:35
  110.9 2.0 copy.127
  112.9 7.6 %gather_fusion.4 = f32[1024,2,16]{2,1,0:T(2,128)} fusion(f32[2,16,3072]{1,0,2:T(2,128)S(1)} %copy.122, s32[1024]{0:T(1024)} %fusion.112), kind=kCustom, calls=%fused_computation.7.clone | custom fusion | bytes 266240 | tf_op jit(solution)/shard_map/jit(_take)/gather | solution.py:35
  122.5 7.6 %gather_fusion.5 = f32[1024,2,16]{2,1,0:T(2,128)} fusion(f32[2,16,3072]{1,0,2:T(2,128)S(1)} %copy.122, s32[1024]{0:T(1024)} %fusion.113), kind=kCustom, calls=%fused_computation.8.clone | custom fusion | bytes 266240 | tf_op jit(solution)/shard_map/jit(_take)/gather | solution.py:35
  132.1 7.6 %gather_fusion.6 = f32[1024,2,16]{2,1,0:T(2,128)} fusion(f32[2,16,3072]{1,0,2:T(2,128)S(1)} %copy.122, s32[1024]{0:T(1024)} %fusion.114), kind=kCustom, calls=%fused_computation.9.clone | custom fusion | bytes 266240 | tf_op jit(solution)/shard_map/jit(_take)/gather | solution.py:35
  141.7 7.5 %gather_fusion.7 = f32[1024,2,16]{2,1,0:T(2,128)} fusion(f32[2,16,3072]{1,0,2:T(2,128)S(1)} %copy.122, s32[1024]{0:T(1024)S(1)} %fusion.115), kind=kCustom, calls=%fused_computation.10.clone | custom fusion | bytes 266240 | tf_op jit(solution)/shard_map/jit(_take)/gather | solution.py:35
  151.2 7.5 %gather_fusion.8 = f32[1024,2,16]{2,1,0:T(2,128)} fusion(f32[2,16,3072]{1,0,2:T(2,128)S(1)} %copy.122, s32[1024]{0:T(1024)S(1)} %fusion.116), kind=kCustom, calls=%fused_computation.11.clone | custom fusion | bytes 266240 | tf_op jit(solution)/shard_map/jit(_take)/gather | solution.py:35
  163.5 22.3 %psum.29 = f32[2,32,16]{1,2,0:T(8,128)S(1)} all-reduce(f32[2,32,16]{1,2,0:T(8,128)S(1)} %convolution_bitcast_fusion.6), channel_id=1, replica_groups=mesh['mesh'=8,'band'=4] {'mesh'}, use_global_device_ids=true, to_apply=%region_1.4 | all-reduce | flops 1024 | bytes 8192 | tf_op jit(solution)/shard_map/psum | solution.py:28
  185.8 14.4 %gather_fusion.9 = f32[2048,2,16]{2,1,0:T(2,128)} fusion(f32[2,16,1024]{1,0,2:T(2,128)S(1)} %copy.138, s32[2048]{0:T(1024)S(1)} %fusion.108), kind=kCustom, calls=%fused_computation.2.clone | custom fusion | bytes 532480 | tf_op jit(solution)/shard_map/jit(_take)/gather | solution.py:29
  200.2 10.0 %broadcast_select_fusion.2 = f32[2048,2,16]{2,1,0:T(2,128)S(1)} fusion(f32[2048,2,16]{2,1,0:T(2,128)} %gather_fusion.9, pred[2048]{0:T(1024)(128)(4,1)S(1)} %copy-done.36), kind=kLoop, calls=%fused_computation.38 | loop fusion | flops 65536 | bytes 526336 | tf_op jit(solution)/shard_map/jit(_take)/select_n | solution.py:29
  212.1 3.6 all-to-all-start.1
  216.3 6.1 %all-to-all-done.1 = f32[2,16,8,256]{3,1,0,2:T(8,128)S(1)} async-done(((f32[2,16,8,256]{3,1,0,2:T(8,128)}), f32[2,16,8,256]{3,1,0,2:T(8,128)S(1)}, u32[]{:S(2)}, u32[]{:S(2)}) %all-to-all-start.1) | async-done | bytes 262176 | tf_op jit(solution)/shard_map/all_to_all | solution.py:30
  223.2 4.1 copy.141
  227.3 7.6 %gather_fusion.10 = f32[1024,2,16]{2,1,0:T(2,128)} fusion(f32[2,16,3072]{1,0,2:T(2,128)S(1)} %copy.141, s32[1024]{0:T(1024)} %fusion.109), kind=kCustom, calls=%fused_computation.12.clone | custom fusion | bytes 266240 | tf_op jit(solution)/shard_map/jit(_take)/gather | solution.py:35
  235.0 7.6 %gather_fusion.11 = f32[1024,2,16]{2,1,0:T(2,128)} fusion(f32[2,16,3072]{1,0,2:T(2,128)S(1)} %copy.141, s32[1024]{0:T(1024)} %fusion.110), kind=kCustom, calls=%fused_computation.13.clone | custom fusion | bytes 266240 | tf_op jit(solution)/shard_map/jit(_take)/gather | solution.py:35
  242.6 7.6 %gather_fusion.12 = f32[1024,2,16]{2,1,0:T(2,128)} fusion(f32[2,16,3072]{1,0,2:T(2,128)S(1)} %copy.141, s32[1024]{0:T(1024)} %fusion.111), kind=kCustom, calls=%fused_computation.14.clone | custom fusion | bytes 266240 | tf_op jit(solution)/shard_map/jit(_take)/gather | solution.py:35
  250.2 7.6 %gather_fusion.13 = f32[1024,2,16]{2,1,0:T(2,128)} fusion(f32[2,16,3072]{1,0,2:T(2,128)S(1)} %copy.141, s32[1024]{0:T(1024)} %fusion.112), kind=kCustom, calls=%fused_computation.15.clone | custom fusion | bytes 266240 | tf_op jit(solution)/shard_map/jit(_take)/gather | solution.py:35
  257.8 7.6 %gather_fusion.14 = f32[1024,2,16]{2,1,0:T(2,128)} fusion(f32[2,16,3072]{1,0,2:T(2,128)S(1)} %copy.141, s32[1024]{0:T(1024)} %fusion.113), kind=kCustom, calls=%fused_computation.16.clone | custom fusion | bytes 266240 | tf_op jit(solution)/shard_map/jit(_take)/gather | solution.py:35
  265.4 7.6 %gather_fusion.15 = f32[1024,2,16]{2,1,0:T(2,128)} fusion(f32[2,16,3072]{1,0,2:T(2,128)S(1)} %copy.141, s32[1024]{0:T(1024)} %fusion.114), kind=kCustom, calls=%fused_computation.17.clone | custom fusion | bytes 266240 | tf_op jit(solution)/shard_map/jit(_take)/gather | solution.py:35
  273.0 7.5 %gather_fusion.16 = f32[1024,2,16]{2,1,0:T(2,128)} fusion(f32[2,16,3072]{1,0,2:T(2,128)S(1)} %copy.141, s32[1024]{0:T(1024)S(1)} %fusion.115), kind=kCustom, calls=%fused_computation.18.clone | custom fusion | bytes 266240 | tf_op jit(solution)/shard_map/jit(_take)/gather | solution.py:35
  280.5 7.5 %gather_fusion.17 = f32[1024,2,16]{2,1,0:T(2,128)} fusion(f32[2,16,3072]{1,0,2:T(2,128)S(1)} %copy.141, s32[1024]{0:T(1024)S(1)} %fusion.116), kind=kCustom, calls=%fused_computation.19.clone | custom fusion | bytes 266240 | tf_op jit(solution)/shard_map/jit(_take)/gather | solution.py:35
  288.0 2.1 copy.142
  290.1 2.1 copy.144
  292.2 2.1 copy.146
  303.7 22.3 %psum.30 = f32[2,32,16]{1,2,0:T(8,128)S(1)} all-reduce(f32[2,32,16]{1,2,0:T(8,128)S(1)} %convolution_bitcast_fusion.5), channel_id=1, replica_groups=mesh['mesh'=8,'band'=4] {'mesh'}, use_global_device_ids=true, to_apply=%region_2.5 | all-reduce | flops 1024 | bytes 8192 | tf_op jit(solution)/shard_map/psum | solution.py:28
  326.0 14.4 %gather_fusion.18 = f32[2048,2,16]{2,1,0:T(2,128)} fusion(f32[2,16,1024]{1,0,2:T(2,128)S(1)} %copy.157, s32[2048]{0:T(1024)S(1)} %fusion.108), kind=kCustom, calls=%fused_computation.3.clone | custom fusion | bytes 532480 | tf_op jit(solution)/shard_map/jit(_take)/gather | solution.py:29
  340.4 10.0 %broadcast_select_fusion.1 = f32[2048,2,16]{2,1,0:T(2,128)S(1)} fusion(f32[2048,2,16]{2,1,0:T(2,128)} %gather_fusion.18, pred[2048]{0:T(1024)(128)(4,1)S(1)} %copy-done.37), kind=kLoop, calls=%fused_computation.37 | loop fusion | flops 65536 | bytes 526336 | tf_op jit(solution)/shard_map/jit(_take)/select_n | solution.py:29
  352.3 3.4 all-to-all-start.2
  356.3 6.2 %all-to-all-done.2 = f32[2,16,8,256]{3,1,0,2:T(8,128)S(1)} async-done(((f32[2,16,8,256]{3,1,0,2:T(8,128)}), f32[2,16,8,256]{3,1,0,2:T(8,128)S(1)}, u32[]{:S(2)}, u32[]{:S(2)}) %all-to-all-start.2) | async-done | bytes 262176 | tf_op jit(solution)/shard_map/all_to_all | solution.py:30
  363.4 4.1 copy.160
  367.5 7.6 %gather_fusion.19 = f32[1024,2,16]{2,1,0:T(2,128)} fusion(f32[2,16,3072]{1,0,2:T(2,128)S(1)} %copy.160, s32[1024]{0:T(1024)} %fusion.109), kind=kCustom, calls=%fused_computation.20.clone | custom fusion | bytes 266240 | tf_op jit(solution)/shard_map/jit(_take)/gather | solution.py:35
  375.2 7.6 %gather_fusion.20 = f32[1024,2,16]{2,1,0:T(2,128)} fusion(f32[2,16,3072]{1,0,2:T(2,128)S(1)} %copy.160, s32[1024]{0:T(1024)} %fusion.110), kind=kCustom, calls=%fused_computation.21.clone | custom fusion | bytes 266240 | tf_op jit(solution)/shard_map/jit(_take)/gather | solution.py:35
  382.8 7.6 %gather_fusion.21 = f32[1024,2,16]{2,1,0:T(2,128)} fusion(f32[2,16,3072]{1,0,2:T(2,128)S(1)} %copy.160, s32[1024]{0:T(1024)} %fusion.111), kind=kCustom, calls=%fused_computation.22.clone | custom fusion | bytes 266240 | tf_op jit(solution)/shard_map/jit(_take)/gather | solution.py:35
  390.4 7.6 %gather_fusion.22 = f32[1024,2,16]{2,1,0:T(2,128)} fusion(f32[2,16,3072]{1,0,2:T(2,128)S(1)} %copy.160, s32[1024]{0:T(1024)} %fusion.112), kind=kCustom, calls=%fused_computation.23.clone | custom fusion | bytes 266240 | tf_op jit(solution)/shard_map/jit(_take)/gather | solution.py:35
  398.0 7.6 %gather_fusion.23 = f32[1024,2,16]{2,1,0:T(2,128)} fusion(f32[2,16,3072]{1,0,2:T(2,128)S(1)} %copy.160, s32[1024]{0:T(1024)} %fusion.113), kind=kCustom, calls=%fused_computation.24.clone | custom fusion | bytes 266240 | tf_op jit(solution)/shard_map/jit(_take)/gather | solution.py:35
  405.6 7.6 %gather_fusion.24 = f32[1024,2,16]{2,1,0:T(2,128)} fusion(f32[2,16,3072]{1,0,2:T(2,128)S(1)} %copy.160, s32[1024]{0:T(1024)} %fusion.114), kind=kCustom, calls=%fused_computation.25.clone | custom fusion | bytes 266240 | tf_op jit(solution)/shard_map/jit(_take)/gather | solution.py:35
  413.2 7.5 %gather_fusion.25 = f32[1024,2,16]{2,1,0:T(2,128)} fusion(f32[2,16,3072]{1,0,2:T(2,128)S(1)} %copy.160, s32[1024]{0:T(1024)S(1)} %fusion.115), kind=kCustom, calls=%fused_computation.26.clone | custom fusion | bytes 266240 | tf_op jit(solution)/shard_map/jit(_take)/gather | solution.py:35
  420.7 7.5 %gather_fusion.26 = f32[1024,2,16]{2,1,0:T(2,128)} fusion(f32[2,16,3072]{1,0,2:T(2,128)S(1)} %copy.160, s32[1024]{0:T(1024)S(1)} %fusion.116), kind=kCustom, calls=%fused_computation.27.clone | custom fusion | bytes 266240 | tf_op jit(solution)/shard_map/jit(_take)/gather | solution.py:35
  428.1 2.1 copy.161
  430.2 2.1 copy.163
  432.4 2.1 copy.165
  443.8 22.3 %psum.31 = f32[2,32,16]{1,2,0:T(8,128)S(1)} all-reduce(f32[2,32,16]{1,2,0:T(8,128)S(1)} %convolution_bitcast_fusion.4), channel_id=1, replica_groups=mesh['mesh'=8,'band'=4] {'mesh'}, use_global_device_ids=true, to_apply=%region_3.6 | all-reduce | flops 1024 | bytes 8192 | tf_op jit(solution)/shard_map/psum | solution.py:28
  466.1 14.4 %gather_fusion.27 = f32[2048,2,16]{2,1,0:T(2,128)} fusion(f32[2,16,1024]{1,0,2:T(2,128)S(1)} %copy.176, s32[2048]{0:T(1024)S(1)} %fusion.108), kind=kCustom, calls=%fused_computation.4.clone | custom fusion | bytes 532480 | tf_op jit(solution)/shard_map/jit(_take)/gather | solution.py:29
  480.6 10.0 %broadcast_select_fusion = f32[2048,2,16]{2,1,0:T(2,128)S(1)} fusion(f32[2048,2,16]{2,1,0:T(2,128)} %gather_fusion.27, pred[2048]{0:T(1024)(128)(4,1)S(1)} %copy-done.38), kind=kLoop, calls=%fused_computation.36 | loop fusion | flops 65536 | bytes 526336 | tf_op jit(solution)/shard_map/jit(_take)/select_n | solution.py:29
  492.4 3.8 all-to-all-start.3
  496.8 6.0 %all-to-all-done.3 = f32[2,16,8,256]{3,1,0,2:T(8,128)S(1)} async-done(((f32[2,16,8,256]{3,1,0,2:T(8,128)}), f32[2,16,8,256]{3,1,0,2:T(8,128)S(1)}, u32[]{:S(2)}, u32[]{:S(2)}) %all-to-all-start.3) | async-done | bytes 262176 | tf_op jit(solution)/shard_map/all_to_all | solution.py:30
  503.7 4.1 copy.179
  507.8 7.6 %gather_fusion.28 = f32[1024,2,16]{2,1,0:T(2,128)} fusion(f32[2,16,3072]{1,0,2:T(2,128)S(1)} %copy.179, s32[1024]{0:T(1024)} %fusion.109), kind=kCustom, calls=%fused_computation.28.clone | custom fusion | bytes 266240 | tf_op jit(solution)/shard_map/jit(_take)/gather | solution.py:35
  515.4 7.6 %gather_fusion.29 = f32[1024,2,16]{2,1,0:T(2,128)} fusion(f32[2,16,3072]{1,0,2:T(2,128)S(1)} %copy.179, s32[1024]{0:T(1024)} %fusion.110), kind=kCustom, calls=%fused_computation.29.clone | custom fusion | bytes 266240 | tf_op jit(solution)/shard_map/jit(_take)/gather | solution.py:35
  523.0 7.6 %gather_fusion.30 = f32[1024,2,16]{2,1,0:T(2,128)} fusion(f32[2,16,3072]{1,0,2:T(2,128)S(1)} %copy.179, s32[1024]{0:T(1024)} %fusion.111), kind=kCustom, calls=%fused_computation.30.clone | custom fusion | bytes 266240 | tf_op jit(solution)/shard_map/jit(_take)/gather | solution.py:35
  530.6 7.6 %gather_fusion.31 = f32[1024,2,16]{2,1,0:T(2,128)} fusion(f32[2,16,3072]{1,0,2:T(2,128)S(1)} %copy.179, s32[1024]{0:T(1024)} %fusion.112), kind=kCustom, calls=%fused_computation.31.clone | custom fusion | bytes 266240 | tf_op jit(solution)/shard_map/jit(_take)/gather | solution.py:35
  538.2 7.5 %gather_fusion.32 = f32[1024,2,16]{2,1,0:T(2,128)} fusion(f32[2,16,3072]{1,0,2:T(2,128)S(1)} %copy.179, s32[1024]{0:T(1024)S(1)} %copy-done.29), kind=kCustom, calls=%fused_computation.32.clone | custom fusion | bytes 266240 | tf_op jit(solution)/shard_map/jit(_take)/gather | solution.py:35
  545.7 7.5 %gather_fusion.33 = f32[1024,2,16]{2,1,0:T(2,128)} fusion(f32[2,16,3072]{1,0,2:T(2,128)S(1)} %copy.179, s32[1024]{0:T(1024)S(1)} %copy-done.28), kind=kCustom, calls=%fused_computation.33.clone | custom fusion | bytes 266240 | tf_op jit(solution)/shard_map/jit(_take)/gather | solution.py:35
  553.2 7.5 %gather_fusion.34 = f32[1024,2,16]{2,1,0:T(2,128)} fusion(f32[2,16,3072]{1,0,2:T(2,128)S(1)} %copy.179, s32[1024]{0:T(1024)S(1)} %fusion.115), kind=kCustom, calls=%fused_computation.34.clone | custom fusion | bytes 266240 | tf_op jit(solution)/shard_map/jit(_take)/gather | solution.py:35
  560.7 7.5 %gather_fusion.35 = f32[1024,2,16]{2,1,0:T(2,128)} fusion(f32[2,16,3072]{1,0,2:T(2,128)S(1)} %copy.179, s32[1024]{0:T(1024)S(1)} %fusion.116), kind=kCustom, calls=%fused_computation.35.clone | custom fusion | bytes 266240 | tf_op jit(solution)/shard_map/jit(_take)/gather | solution.py:35
  568.2 2.2 copy.180
  (178 shorter events, 69.4 us)
Async XLA Ops:
  0.7 27.7 %copy-start.35 = (pred[2048]{0:T(1024)(128)(4,1)}, pred[2048]{0:T(1024)(128)(4,1)S(1)}, u32[]{:S(2)}) copy-start(pred[2048]{0:T(1024)(128)(4,1)S(1)} %compare_and_fusion) | copy-start | bytes 6148
  16.5 17.1 %copy-start = (f32[2,16,1024]{2,1,0:T(8,128)S(1)}, f32[2,16,1024]{2,1,0:T(8,128)}, u32[]{:S(2)}) copy-start(f32[2,16,1024]{2,1,0:T(8,128)} %param.10) | copy-start | bytes 393220
  16.5 17.1 %copy-start.39 = (s32[8,1024]{1,0:T(8,128)S(1)}, s32[8,1024]{1,0:T(8,128)}, u32[]{:S(2)}) copy-start(s32[8,1024]{1,0:T(8,128)} %param.15) | copy-start | bytes 98308
  16.5 23.1 %copy-start.34 = (f32[2,8,1024]{2,1,0:T(8,128)S(1)}, f32[2,8,1024]{2,1,0:T(8,128)}, u32[]{:S(2)}) copy-start(f32[2,8,1024]{2,1,0:T(8,128)} %param.11) | copy-start | bytes 196612
  26.5 50.7 %copy-start.41 = (f32[1024]{0:T(1024)S(1)}, f32[1024]{0:T(1024)}, u32[]{:S(2)}) copy-start(f32[1024]{0:T(1024)} %param.13) | copy-start | bytes 12292
  26.6 51.9 %copy-start.40 = (f32[8,1024]{1,0:T(8,128)S(1)}, f32[8,1024]{1,0:T(8,128)}, u32[]{:S(2)}) copy-start(f32[8,1024]{1,0:T(8,128)} %param.12) | copy-start | bytes 98308
  28.5 50.6 %all-to-all-start = ((f32[2,16,8,256]{3,1,0,2:T(8,128)}), f32[2,16,8,256]{3,1,0,2:T(8,128)S(1)}, u32[]{:S(2)}, u32[]{:S(2)}) async-start(f32[2,16,8,256]{3,1,0,2:T(8,128)} %copy.120), calls=%async_computation | async-start | bytes 524288 | tf_op jit(solution)/shard_map/all_to_all | solution.py:30
  158.7 41.6 %copy-start.36 = (pred[2048]{0:T(1024)(128)(4,1)S(1)}, pred[2048]{0:T(1024)(128)(4,1)}, u32[]{:S(2)}) copy-start(pred[2048]{0:T(1024)(128)(4,1)} %copy-done.35) | copy-start | bytes 6148
  161.9 0.6 copy-start.11
  161.9 0.6 copy-start.13
  212.1 10.3 %all-to-all-start.1 = ((f32[2,16,8,256]{3,1,0,2:T(8,128)}), f32[2,16,8,256]{3,1,0,2:T(8,128)S(1)}, u32[]{:S(2)}, u32[]{:S(2)}) async-start(f32[2,16,8,256]{3,1,0,2:T(8,128)} %copy.139), calls=%async_computation.1 | async-start | bytes 524288 | tf_op jit(solution)/shard_map/all_to_all | solution.py:30
  287.9 10.4 %copy-start.9 = (f32[1024,2,16]{2,1,0:T(2,128)S(1)}, f32[1024,2,16]{2,1,0:T(2,128)}, u32[]{:S(2)}) copy-start(f32[1024,2,16]{2,1,0:T(2,128)} %gather_fusion.15) | copy-start | bytes 393220
  290.0 9.3 %copy-start.7 = (f32[1024,2,16]{2,1,0:T(2,128)S(1)}, f32[1024,2,16]{2,1,0:T(2,128)}, u32[]{:S(2)}) copy-start(f32[1024,2,16]{2,1,0:T(2,128)} %gather_fusion.16) | copy-start | bytes 393220
  292.2 7.6 %copy-start.5 = (f32[1024,2,16]{2,1,0:T(2,128)S(1)}, f32[1024,2,16]{2,1,0:T(2,128)}, u32[]{:S(2)}) copy-start(f32[1024,2,16]{2,1,0:T(2,128)} %gather_fusion.17) | copy-start | bytes 393220
  299.8 40.6 %copy-start.37 = (pred[2048]{0:T(1024)(128)(4,1)S(1)}, pred[2048]{0:T(1024)(128)(4,1)}, u32[]{:S(2)}) copy-start(pred[2048]{0:T(1024)(128)(4,1)} %copy-done.35) | copy-start | bytes 6148
  302.1 0.6 copy-start.15
  302.1 0.6 copy-start.17
  352.3 10.3 %all-to-all-start.2 = ((f32[2,16,8,256]{3,1,0,2:T(8,128)}), f32[2,16,8,256]{3,1,0,2:T(8,128)S(1)}, u32[]{:S(2)}, u32[]{:S(2)}) async-start(f32[2,16,8,256]{3,1,0,2:T(8,128)} %copy.158), calls=%async_computation.2 | async-start | bytes 524288 | tf_op jit(solution)/shard_map/all_to_all | solution.py:30
  428.1 10.4 %copy-start.10 = (f32[1024,2,16]{2,1,0:T(2,128)S(1)}, f32[1024,2,16]{2,1,0:T(2,128)}, u32[]{:S(2)}) copy-start(f32[1024,2,16]{2,1,0:T(2,128)} %gather_fusion.24) | copy-start | bytes 393220
  430.2 9.3 %copy-start.8 = (f32[1024,2,16]{2,1,0:T(2,128)S(1)}, f32[1024,2,16]{2,1,0:T(2,128)}, u32[]{:S(2)}) copy-start(f32[1024,2,16]{2,1,0:T(2,128)} %gather_fusion.25) | copy-start | bytes 393220
  432.4 7.6 %copy-start.6 = (f32[1024,2,16]{2,1,0:T(2,128)S(1)}, f32[1024,2,16]{2,1,0:T(2,128)}, u32[]{:S(2)}) copy-start(f32[1024,2,16]{2,1,0:T(2,128)} %gather_fusion.26) | copy-start | bytes 393220
  440.0 40.6 %copy-start.38 = (pred[2048]{0:T(1024)(128)(4,1)S(1)}, pred[2048]{0:T(1024)(128)(4,1)}, u32[]{:S(2)}) copy-start(pred[2048]{0:T(1024)(128)(4,1)} %copy-done.35) | copy-start | bytes 6148
  442.2 0.6 copy-start.19
  442.2 0.6 copy-start.21
  492.4 45.7 %copy-start.29 = (s32[1024]{0:T(1024)S(1)}, s32[1024]{0:T(1024)}, u32[]{:S(2)}) copy-start(s32[1024]{0:T(1024)} %fusion.113) | copy-start | bytes 12292
  492.4 10.4 %all-to-all-start.3 = ((f32[2,16,8,256]{3,1,0,2:T(8,128)}), f32[2,16,8,256]{3,1,0,2:T(8,128)S(1)}, u32[]{:S(2)}, u32[]{:S(2)}) async-start(f32[2,16,8,256]{3,1,0,2:T(8,128)} %copy.177), calls=%async_computation.3 | async-start | bytes 524288 | tf_op jit(solution)/shard_map/all_to_all | solution.py:30
  496.2 49.5 %copy-start.28 = (s32[1024]{0:T(1024)S(1)}, s32[1024]{0:T(1024)}, u32[]{:S(2)}) copy-start(s32[1024]{0:T(1024)} %fusion.114) | copy-start | bytes 12292
  568.2 6.2 %copy-start.1 = (f32[1024,2,16]{2,1,0:T(2,128)S(1)}, f32[1024,2,16]{2,1,0:T(2,128)}, u32[]{:S(2)}) copy-start(f32[1024,2,16]{2,1,0:T(2,128)} %gather_fusion.31) | copy-start | bytes 393220
  568.2 7.3 %copy-start.2 = (f32[1024,2,16]{2,1,0:T(2,128)S(1)}, f32[1024,2,16]{2,1,0:T(2,128)}, u32[]{:S(2)}) copy-start(f32[1024,2,16]{2,1,0:T(2,128)} %gather_fusion.32) | copy-start | bytes 393220
  568.2 8.4 %copy-start.3 = (f32[1024,2,16]{2,1,0:T(2,128)S(1)}, f32[1024,2,16]{2,1,0:T(2,128)}, u32[]{:S(2)}) copy-start(f32[1024,2,16]{2,1,0:T(2,128)} %gather_fusion.33) | copy-start | bytes 393220
  574.4 5.2 copy-start.30
  574.4 5.2 copy-start.31
  574.4 5.2 copy-start.32
  574.4 5.2 copy-start.33
  575.5 3.6 copy-start.4
  576.6 3.0 copy-start.20
  576.6 3.0 copy-start.22
  576.6 3.0 copy-start.23
  576.6 3.0 copy-start.24
  576.6 3.0 copy-start.25
  576.6 3.0 copy-start.26
  576.6 3.0 copy-start.27
  576.6 4.5 copy-start.12
  576.7 4.5 copy-start.14
  576.7 4.5 copy-start.16
  576.7 4.5 copy-start.18
where the time goes:
time: 585 us; the launch traced here: 582 us
  local copies, waits for them, and re-layouts  382 us (65%)
  blocking collectives  104 us (18%)
  other arithmetic  53 us (9%)
  waiting for transfers between devices  18.3 us (3%)
  starting transfers between devices  15.9 us (3%)
  matrix products  8.07 us (1%)
    gather x64, local copies, waits for them, and re-layouts, body(): jnp.take(extended, neighbours[apply_order], axis=2) - term  293 us
    psum x4, blocking collectives, body(): intersection = lax.psum(partial_intersection, 'mesh')  89.9 us
    gather x4, local copies, waits for them, and re-layouts, body(): jnp.take(term, routes.reshape(-1), axis=2).reshape(2, rows, parts, capacity)  57.7 us
    select_n x4, other arithmetic, body(): jnp.take(term, routes.reshape(-1), axis=2).reshape(2, rows, parts, capacity)  39.9 us
    all_to_all x4, waiting for transfers between devices, body(): lax.all_to_all(packed, 'mesh', split_axis=2, concat_axis=2, tiled=True)  18.3 us
    concatenate x4, local copies, waits for them, and re-layouts, body(): jnp.concatenate([term, arrived.reshape(2, rows, parts * capacity)], axis=2)  16.6 us
    all_to_all x4, starting transfers between devices, body(): lax.all_to_all(packed, 'mesh', split_axis=2, concat_axis=2, tiled=True)  15.9 us
    all_gather x1, blocking collectives, body(): full_frozen = lax.all_gather(frozen, 'band', axis=1, tiled=True)  14.2 us
  transfers between devices with their start and end apart: 4, of which 3 were waited for; matrix products, arithmetic and copies ran while one was open for 2% of the time, Pallas kernels for 0%

commit v1 on v0

--- a/solution.py
+++ b/solution.py
@@ -25,7 +25,8 @@
         partial_intersection = jnp.einsum(
             "cmp,ocjp->omj", full_frozen, paired, precision=lax.Precision.HIGHEST
         )
-        intersection = lax.psum(partial_intersection, "mesh")
+        pieces = lax.all_gather(partial_intersection, "mesh")
+        intersection = jnp.sum(pieces, axis=0)
         packed = jnp.take(term, routes.reshape(-1), axis=2).reshape(2, rows, parts, capacity)
         arrived = lax.all_to_all(packed, "mesh", split_axis=2, concat_axis=2, tiled=True)
         extended = jnp.concatenate([term, arrived.reshape(2, rows, parts * capacity)], axis=2)

time: 585 us -> 530 us (0.906)
  blocking collectives: 104 us -> 49.4 us
    psum x4 -> x0, blocking collectives: 89.9 us -> none  [body(): intersection = lax.psum(partial_intersection, 'mesh')]
    all_gather x0 -> x4, blocking collectives: none -> 35.2 us  [body(): pieces = lax.all_gather(partial_intersection, 'mesh')]
where the time goes in v1:
time: 530 us; the launch traced here: 527 us
  local copies, waits for them, and re-layouts  382 us (72%)
  other arithmetic  53 us (10%)
  blocking collectives  49.4 us (9%)
  waiting for transfers between devices  18.3 us (3%)
  starting transfers between devices  15.9 us (3%)
  matrix products  8.06 us (2%)
    gather x64, local copies, waits for them, and re-layouts, body(): jnp.take(extended, neighbours[apply_order], axis=2) - term  293 us
    gather x4, local copies, waits for them, and re-layouts, body(): jnp.take(term, routes.reshape(-1), axis=2).reshape(2, rows, parts, capacity)  57.7 us
    select_n x4, other arithmetic, body(): jnp.take(term, routes.reshape(-1), axis=2).reshape(2, rows, parts, capacity)  39.9 us
    all_gather x4, blocking collectives, body(): pieces = lax.all_gather(partial_intersection, 'mesh')  35.2 us
    all_to_all x4, waiting for transfers between devices, body(): lax.all_to_all(packed, 'mesh', split_axis=2, concat_axis=2, tiled=True)  18.3 us
    concatenate x4, local copies, waits for them, and re-layouts, body(): jnp.concatenate([term, arrived.reshape(2, rows, parts * capacity)], axis=2)  16.6 us
    all_to_all x4, starting transfers between devices, body(): lax.all_to_all(packed, 'mesh', split_axis=2, concat_axis=2, tiled=True)  15.9 us
    all_gather x1, blocking collectives, body(): full_frozen = lax.all_gather(frozen, 'band', axis=1, tiled=True)  14.2 us
  transfers between devices with their start and end apart: 4, of which 3 were waited for; matrix products, arithmetic and copies ran while one was open for 2% of the time, Pallas kernels for 0%

profile of v1, /device:TPU:0, one launch (start us, length us, event | category | flops | bytes accessed | tf_op | source)
XLA Modules:
  0.0 527.3 jit_solution(10465270733937517783)
XLA Ops:
  2.1 14.4 %gather_fusion = f32[2048,2,16]{2,1,0:T(2,128)} fusion(f32[2,16,1024]{1,0,2:T(2,128)S(1)} %copy.119, s32[2048]{0:T(1024)S(1)} %fusion.108), kind=kCustom, calls=%fused_computation.clone | custom fusion | bytes 532480 | tf_op jit(solution)/shard_map/jit(_take)/gather | solution.py:30
  16.5 10.0 %broadcast_select_fusion.3 = f32[2048,2,16]{2,1,0:T(2,128)S(1)} fusion(f32[2048,2,16]{2,1,0:T(2,128)} %gather_fusion, pred[2048]{0:T(1024)(128)(4,1)S(1)} %compare_and_fusion), kind=kLoop, calls=%fused_computation.39 | loop fusion | flops 65536 | bytes 526336 | tf_op jit(solution)/shard_map/jit(_take)/select_n | solution.py:30
  28.5 5.2 all-to-all-start
  39.6 14.2 %all_gather.27 = f32[2,32,1024]{2,1,0:T(8,128)S(1)} all-gather(f32[2,8,1024]{2,1,0:T(8,128)S(1)} %copy-done.34), channel_id=1, replica_groups=mesh['mesh'=8,'band'=4] {'band'}, dimensions={1}, use_global_device_ids=true | all-gather | bytes 327680 | tf_op jit(solution)/shard_map/all_gather | solution.py:20
  54.3 9.5 %all-gather = f32[16,32,16]{1,2,0:T(8,128)S(1)} all-gather(f32[2,32,16]{1,2,0:T(8,128)S(1)} %convolution_bitcast_fusion.7), channel_id=2, replica_groups=mesh['mesh'=8,'band'=4] {'mesh'}, dimensions={0}, use_global_device_ids=true | all-gather | bytes 36864 | tf_op jit(solution)/shard_map/all_gather | solution.py:28
  66.4 4.1 copy.122
  70.6 7.6 %gather_fusion.1 = f32[1024,2,16]{2,1,0:T(2,128)} fusion(f32[2,16,3072]{1,0,2:T(2,128)S(1)} %copy.122, s32[1024]{0:T(1024)} %fusion.109), kind=kCustom, calls=%fused_computation.1.clone | custom fusion | bytes 266240 | tf_op jit(solution)/shard_map/jit(_take)/gather | solution.py:36
  80.2 7.6 %gather_fusion.2 = f32[1024,2,16]{2,1,0:T(2,128)} fusion(f32[2,16,3072]{1,0,2:T(2,128)S(1)} %copy.122, s32[1024]{0:T(1024)} %fusion.110), kind=kCustom, calls=%fused_computation.5.clone | custom fusion | bytes 266240 | tf_op jit(solution)/shard_map/jit(_take)/gather | solution.py:36
  89.8 7.6 %gather_fusion.3 = f32[1024,2,16]{2,1,0:T(2,128)} fusion(f32[2,16,3072]{1,0,2:T(2,128)S(1)} %copy.122, s32[1024]{0:T(1024)} %fusion.111), kind=kCustom, calls=%fused_computation.6.clone | custom fusion | bytes 266240 | tf_op jit(solution)/shard_map/jit(_take)/gather | solution.py:36
  97.4 2.0 copy.127
  99.4 7.6 %gather_fusion.4 = f32[1024,2,16]{2,1,0:T(2,128)} fusion(f32[2,16,3072]{1,0,2:T(2,128)S(1)} %copy.122, s32[1024]{0:T(1024)} %fusion.112), kind=kCustom, calls=%fused_computation.7.clone | custom fusion | bytes 266240 | tf_op jit(solution)/shard_map/jit(_take)/gather | solution.py:36
  109.1 7.6 %gather_fusion.5 = f32[1024,2,16]{2,1,0:T(2,128)} fusion(f32[2,16,3072]{1,0,2:T(2,128)S(1)} %copy.122, s32[1024]{0:T(1024)} %fusion.113), kind=kCustom, calls=%fused_computation.8.clone | custom fusion | bytes 266240 | tf_op jit(solution)/shard_map/jit(_take)/gather | solution.py:36
  118.7 7.6 %gather_fusion.6 = f32[1024,2,16]{2,1,0:T(2,128)} fusion(f32[2,16,3072]{1,0,2:T(2,128)S(1)} %copy.122, s32[1024]{0:T(1024)} %fusion.114), kind=kCustom, calls=%fused_computation.9.clone | custom fusion | bytes 266240 | tf_op jit(solution)/shard_map/jit(_take)/gather | solution.py:36
  128.3 7.5 %gather_fusion.7 = f32[1024,2,16]{2,1,0:T(2,128)} fusion(f32[2,16,3072]{1,0,2:T(2,128)S(1)} %copy.122, s32[1024]{0:T(1024)S(1)} %fusion.115), kind=kCustom, calls=%fused_computation.10.clone | custom fusion | bytes 266240 | tf_op jit(solution)/shard_map/jit(_take)/gather | solution.py:36
  137.8 7.5 %gather_fusion.8 = f32[1024,2,16]{2,1,0:T(2,128)} fusion(f32[2,16,3072]{1,0,2:T(2,128)S(1)} %copy.122, s32[1024]{0:T(1024)S(1)} %fusion.116), kind=kCustom, calls=%fused_computation.11.clone | custom fusion | bytes 266240 | tf_op jit(solution)/shard_map/jit(_take)/gather | solution.py:36
  150.0 9.2 %all-gather.1 = f32[16,32,16]{1,2,0:T(8,128)S(1)} all-gather(f32[2,32,16]{1,2,0:T(8,128)S(1)} %convolution_bitcast_fusion.6), channel_id=3, replica_groups=mesh['mesh'=8,'band'=4] {'mesh'}, dimensions={0}, use_global_device_ids=true | all-gather | bytes 36864 | tf_op jit(solution)/shard_map/all_gather | solution.py:28
  159.3 14.4 %gather_fusion.9 = f32[2048,2,16]{2,1,0:T(2,128)} fusion(f32[2,16,1024]{1,0,2:T(2,128)S(1)} %copy.138, s32[2048]{0:T(1024)S(1)} %fusion.108), kind=kCustom, calls=%fused_computation.2.clone | custom fusion | bytes 532480 | tf_op jit(solution)/shard_map/jit(_take)/gather | solution.py:30
  173.7 10.0 %broadcast_select_fusion.2 = f32[2048,2,16]{2,1,0:T(2,128)S(1)} fusion(f32[2048,2,16]{2,1,0:T(2,128)} %gather_fusion.9, pred[2048]{0:T(1024)(128)(4,1)S(1)} %copy-done.36), kind=kLoop, calls=%fused_computation.38 | loop fusion | flops 65536 | bytes 526336 | tf_op jit(solution)/shard_map/jit(_take)/select_n | solution.py:30
  185.6 3.6 all-to-all-start.1
  189.8 6.1 %all-to-all-done.1 = f32[2,16,8,256]{3,1,0,2:T(8,128)S(1)} async-done(((f32[2,16,8,256]{3,1,0,2:T(8,128)}), f32[2,16,8,256]{3,1,0,2:T(8,128)S(1)}, u32[]{:S(2)}, u32[]{:S(2)}) %all-to-all-start.1) | async-done | bytes 262176 | tf_op jit(solution)/shard_map/all_to_all | solution.py:31
  196.6 4.1 copy.141
  200.8 7.6 %gather_fusion.10 = f32[1024,2,16]{2,1,0:T(2,128)} fusion(f32[2,16,3072]{1,0,2:T(2,128)S(1)} %copy.141, s32[1024]{0:T(1024)} %fusion.109), kind=kCustom, calls=%fused_computation.12.clone | custom fusion | bytes 266240 | tf_op jit(solution)/shard_map/jit(_take)/gather | solution.py:36
  208.4 7.6 %gather_fusion.11 = f32[1024,2,16]{2,1,0:T(2,128)} fusion(f32[2,16,3072]{1,0,2:T(2,128)S(1)} %copy.141, s32[1024]{0:T(1024)} %fusion.110), kind=kCustom, calls=%fused_computation.13.clone | custom fusion | bytes 266240 | tf_op jit(solution)/shard_map/jit(_take)/gather | solution.py:36
  216.0 7.6 %gather_fusion.12 = f32[1024,2,16]{2,1,0:T(2,128)} fusion(f32[2,16,3072]{1,0,2:T(2,128)S(1)} %copy.141, s32[1024]{0:T(1024)} %fusion.111), kind=kCustom, calls=%fused_computation.14.clone | custom fusion | bytes 266240 | tf_op jit(solution)/shard_map/jit(_take)/gather | solution.py:36
  223.6 7.6 %gather_fusion.13 = f32[1024,2,16]{2,1,0:T(2,128)} fusion(f32[2,16,3072]{1,0,2:T(2,128)S(1)} %copy.141, s32[1024]{0:T(1024)} %fusion.112), kind=kCustom, calls=%fused_computation.15.clone | custom fusion | bytes 266240 | tf_op jit(solution)/shard_map/jit(_take)/gather | solution.py:36
  231.3 7.6 %gather_fusion.14 = f32[1024,2,16]{2,1,0:T(2,128)} fusion(f32[2,16,3072]{1,0,2:T(2,128)S(1)} %copy.141, s32[1024]{0:T(1024)} %fusion.113), kind=kCustom, calls=%fused_computation.16.clone | custom fusion | bytes 266240 | tf_op jit(solution)/shard_map/jit(_take)/gather | solution.py:36
  238.9 7.6 %gather_fusion.15 = f32[1024,2,16]{2,1,0:T(2,128)} fusion(f32[2,16,3072]{1,0,2:T(2,128)S(1)} %copy.141, s32[1024]{0:T(1024)} %fusion.114), kind=kCustom, calls=%fused_computation.17.clone | custom fusion | bytes 266240 | tf_op jit(solution)/shard_map/jit(_take)/gather | solution.py:36
  246.5 7.5 %gather_fusion.16 = f32[1024,2,16]{2,1,0:T(2,128)} fusion(f32[2,16,3072]{1,0,2:T(2,128)S(1)} %copy.141, s32[1024]{0:T(1024)S(1)} %fusion.115), kind=kCustom, calls=%fused_computation.18.clone | custom fusion | bytes 266240 | tf_op jit(solution)/shard_map/jit(_take)/gather | solution.py:36
  253.9 7.5 %gather_fusion.17 = f32[1024,2,16]{2,1,0:T(2,128)} fusion(f32[2,16,3072]{1,0,2:T(2,128)S(1)} %copy.141, s32[1024]{0:T(1024)S(1)} %fusion.116), kind=kCustom, calls=%fused_computation.19.clone | custom fusion | bytes 266240 | tf_op jit(solution)/shard_map/jit(_take)/gather | solution.py:36
  261.4 2.1 copy.142
  263.5 2.1 copy.144
  265.6 2.1 copy.146
  277.1 8.3 %all-gather.2 = f32[16,32,16]{1,2,0:T(8,128)S(1)} all-gather(f32[2,32,16]{1,2,0:T(8,128)S(1)} %convolution_bitcast_fusion.5), channel_id=4, replica_groups=mesh['mesh'=8,'band'=4] {'mesh'}, dimensions={0}, use_global_device_ids=true | all-gather | bytes 36864 | tf_op jit(solution)/shard_map/all_gather | solution.py:28
  285.4 14.4 %gather_fusion.18 = f32[2048,2,16]{2,1,0:T(2,128)} fusion(f32[2,16,1024]{1,0,2:T(2,128)S(1)} %copy.157, s32[2048]{0:T(1024)S(1)} %fusion.108), kind=kCustom, calls=%fused_computation.3.clone | custom fusion | bytes 532480 | tf_op jit(solution)/shard_map/jit(_take)/gather | solution.py:30
  299.8 10.0 %broadcast_select_fusion.1 = f32[2048,2,16]{2,1,0:T(2,128)S(1)} fusion(f32[2048,2,16]{2,1,0:T(2,128)} %gather_fusion.18, pred[2048]{0:T(1024)(128)(4,1)S(1)} %copy-done.37), kind=kLoop, calls=%fused_computation.37 | loop fusion | flops 65536 | bytes 526336 | tf_op jit(solution)/shard_map/jit(_take)/select_n | solution.py:30
  311.7 3.4 all-to-all-start.2
  315.7 6.2 %all-to-all-done.2 = f32[2,16,8,256]{3,1,0,2:T(8,128)S(1)} async-done(((f32[2,16,8,256]{3,1,0,2:T(8,128)}), f32[2,16,8,256]{3,1,0,2:T(8,128)S(1)}, u32[]{:S(2)}, u32[]{:S(2)}) %all-to-all-start.2) | async-done | bytes 262176 | tf_op jit(solution)/shard_map/all_to_all | solution.py:31
  322.8 4.1 copy.160
  326.9 7.6 %gather_fusion.19 = f32[1024,2,16]{2,1,0:T(2,128)} fusion(f32[2,16,3072]{1,0,2:T(2,128)S(1)} %copy.160, s32[1024]{0:T(1024)} %fusion.109), kind=kCustom, calls=%fused_computation.20.clone | custom fusion | bytes 266240 | tf_op jit(solution)/shard_map/jit(_take)/gather | solution.py:36
  334.6 7.6 %gather_fusion.20 = f32[1024,2,16]{2,1,0:T(2,128)} fusion(f32[2,16,3072]{1,0,2:T(2,128)S(1)} %copy.160, s32[1024]{0:T(1024)} %fusion.110), kind=kCustom, calls=%fused_computation.21.clone | custom fusion | bytes 266240 | tf_op jit(solution)/shard_map/jit(_take)/gather | solution.py:36
  342.2 7.6 %gather_fusion.21 = f32[1024,2,16]{2,1,0:T(2,128)} fusion(f32[2,16,3072]{1,0,2:T(2,128)S(1)} %copy.160, s32[1024]{0:T(1024)} %fusion.111), kind=kCustom, calls=%fused_computation.22.clone | custom fusion | bytes 266240 | tf_op jit(solution)/shard_map/jit(_take)/gather | solution.py:36
  349.8 7.6 %gather_fusion.22 = f32[1024,2,16]{2,1,0:T(2,128)} fusion(f32[2,16,3072]{1,0,2:T(2,128)S(1)} %copy.160, s32[1024]{0:T(1024)} %fusion.112), kind=kCustom, calls=%fused_computation.23.clone | custom fusion | bytes 266240 | tf_op jit(solution)/shard_map/jit(_take)/gather | solution.py:36
  357.4 7.6 %gather_fusion.23 = f32[1024,2,16]{2,1,0:T(2,128)} fusion(f32[2,16,3072]{1,0,2:T(2,128)S(1)} %copy.160, s32[1024]{0:T(1024)} %fusion.113), kind=kCustom, calls=%fused_computation.24.clone | custom fusion | bytes 266240 | tf_op jit(solution)/shard_map/jit(_take)/gather | solution.py:36
  365.0 7.6 %gather_fusion.24 = f32[1024,2,16]{2,1,0:T(2,128)} fusion(f32[2,16,3072]{1,0,2:T(2,128)S(1)} %copy.160, s32[1024]{0:T(1024)} %fusion.114), kind=kCustom, calls=%fused_computation.25.clone | custom fusion | bytes 266240 | tf_op jit(solution)/shard_map/jit(_take)/gather | solution.py:36
  372.6 7.5 %gather_fusion.25 = f32[1024,2,16]{2,1,0:T(2,128)} fusion(f32[2,16,3072]{1,0,2:T(2,128)S(1)} %copy.160, s32[1024]{0:T(1024)S(1)} %fusion.115), kind=kCustom, calls=%fused_computation.26.clone | custom fusion | bytes 266240 | tf_op jit(solution)/shard_map/jit(_take)/gather | solution.py:36
  380.1 7.5 %gather_fusion.26 = f32[1024,2,16]{2,1,0:T(2,128)} fusion(f32[2,16,3072]{1,0,2:T(2,128)S(1)} %copy.160, s32[1024]{0:T(1024)S(1)} %fusion.116), kind=kCustom, calls=%fused_computation.27.clone | custom fusion | bytes 266240 | tf_op jit(solution)/shard_map/jit(_take)/gather | solution.py:36
  387.6 2.1 copy.161
  389.7 2.1 copy.163
  391.8 2.1 copy.165
  403.3 8.3 %all-gather.3 = f32[16,32,16]{1,2,0:T(8,128)S(1)} all-gather(f32[2,32,16]{1,2,0:T(8,128)S(1)} %convolution_bitcast_fusion.4), channel_id=5, replica_groups=mesh['mesh'=8,'band'=4] {'mesh'}, dimensions={0}, use_global_device_ids=true | all-gather | bytes 36864 | tf_op jit(solution)/shard_map/all_gather | solution.py:28
  411.5 14.4 %gather_fusion.27 = f32[2048,2,16]{2,1,0:T(2,128)} fusion(f32[2,16,1024]{1,0,2:T(2,128)S(1)} %copy.176, s32[2048]{0:T(1024)S(1)} %fusion.108), kind=kCustom, calls=%fused_computation.4.clone | custom fusion | bytes 532480 | tf_op jit(solution)/shard_map/jit(_take)/gather | solution.py:30
  426.0 10.0 %broadcast_select_fusion = f32[2048,2,16]{2,1,0:T(2,128)S(1)} fusion(f32[2048,2,16]{2,1,0:T(2,128)} %gather_fusion.27, pred[2048]{0:T(1024)(128)(4,1)S(1)} %copy-done.38), kind=kLoop, calls=%fused_computation.36 | loop fusion | flops 65536 | bytes 526336 | tf_op jit(solution)/shard_map/jit(_take)/select_n | solution.py:30
  437.8 3.8 all-to-all-start.3
  442.2 6.0 %all-to-all-done.3 = f32[2,16,8,256]{3,1,0,2:T(8,128)S(1)} async-done(((f32[2,16,8,256]{3,1,0,2:T(8,128)}), f32[2,16,8,256]{3,1,0,2:T(8,128)S(1)}, u32[]{:S(2)}, u32[]{:S(2)}) %all-to-all-start.3) | async-done | bytes 262176 | tf_op jit(solution)/shard_map/all_to_all | solution.py:31
  449.1 4.1 copy.179
  453.2 7.6 %gather_fusion.28 = f32[1024,2,16]{2,1,0:T(2,128)} fusion(f32[2,16,3072]{1,0,2:T(2,128)S(1)} %copy.179, s32[1024]{0:T(1024)} %fusion.109), kind=kCustom, calls=%fused_computation.28.clone | custom fusion | bytes 266240 | tf_op jit(solution)/shard_map/jit(_take)/gather | solution.py:36
  460.8 7.6 %gather_fusion.29 = f32[1024,2,16]{2,1,0:T(2,128)} fusion(f32[2,16,3072]{1,0,2:T(2,128)S(1)} %copy.179, s32[1024]{0:T(1024)} %fusion.110), kind=kCustom, calls=%fused_computation.29.clone | custom fusion | bytes 266240 | tf_op jit(solution)/shard_map/jit(_take)/gather | solution.py:36
  468.4 7.6 %gather_fusion.30 = f32[1024,2,16]{2,1,0:T(2,128)} fusion(f32[2,16,3072]{1,0,2:T(2,128)S(1)} %copy.179, s32[1024]{0:T(1024)} %fusion.111), kind=kCustom, calls=%fused_computation.30.clone | custom fusion | bytes 266240 | tf_op jit(solution)/shard_map/jit(_take)/gather | solution.py:36
  476.0 7.6 %gather_fusion.31 = f32[1024,2,16]{2,1,0:T(2,128)} fusion(f32[2,16,3072]{1,0,2:T(2,128)S(1)} %copy.179, s32[1024]{0:T(1024)} %fusion.112), kind=kCustom, calls=%fused_computation.31.clone | custom fusion | bytes 266240 | tf_op jit(solution)/shard_map/jit(_take)/gather | solution.py:36
  483.6 7.5 %gather_fusion.32 = f32[1024,2,16]{2,1,0:T(2,128)} fusion(f32[2,16,3072]{1,0,2:T(2,128)S(1)} %copy.179, s32[1024]{0:T(1024)S(1)} %copy-done.29), kind=kCustom, calls=%fused_computation.32.clone | custom fusion | bytes 266240 | tf_op jit(solution)/shard_map/jit(_take)/gather | solution.py:36
  491.1 7.5 %gather_fusion.33 = f32[1024,2,16]{2,1,0:T(2,128)} fusion(f32[2,16,3072]{1,0,2:T(2,128)S(1)} %copy.179, s32[1024]{0:T(1024)S(1)} %copy-done.28), kind=kCustom, calls=%fused_computation.33.clone | custom fusion | bytes 266240 | tf_op jit(solution)/shard_map/jit(_take)/gather | solution.py:36
  498.6 7.5 %gather_fusion.34 = f32[1024,2,16]{2,1,0:T(2,128)} fusion(f32[2,16,3072]{1,0,2:T(2,128)S(1)} %copy.179, s32[1024]{0:T(1024)S(1)} %fusion.115), kind=kCustom, calls=%fused_computation.34.clone | custom fusion | bytes 266240 | tf_op jit(solution)/shard_map/jit(_take)/gather | solution.py:36
  506.1 7.5 %gather_fusion.35 = f32[1024,2,16]{2,1,0:T(2,128)} fusion(f32[2,16,3072]{1,0,2:T(2,128)S(1)} %copy.179, s32[1024]{0:T(1024)S(1)} %fusion.116), kind=kCustom, calls=%fused_computation.35.clone | custom fusion | bytes 266240 | tf_op jit(solution)/shard_map/jit(_take)/gather | solution.py:36
  513.6 2.2 copy.180
  (182 shorter events, 69.5 us)
Async XLA Ops:
  0.7 27.7 %copy-start.35 = (pred[2048]{0:T(1024)(128)(4,1)}, pred[2048]{0:T(1024)(128)(4,1)S(1)}, u32[]{:S(2)}) copy-start(pred[2048]{0:T(1024)(128)(4,1)S(1)} %compare_and_fusion) | copy-start | bytes 6148
  16.5 17.1 %copy-start = (f32[2,16,1024]{2,1,0:T(8,128)S(1)}, f32[2,16,1024]{2,1,0:T(8,128)}, u32[]{:S(2)}) copy-start(f32[2,16,1024]{2,1,0:T(8,128)} %param.10) | copy-start | bytes 393220
  16.5 17.1 %copy-start.39 = (s32[8,1024]{1,0:T(8,128)S(1)}, s32[8,1024]{1,0:T(8,128)}, u32[]{:S(2)}) copy-start(s32[8,1024]{1,0:T(8,128)} %param.15) | copy-start | bytes 98308
  16.5 23.1 %copy-start.34 = (f32[2,8,1024]{2,1,0:T(8,128)S(1)}, f32[2,8,1024]{2,1,0:T(8,128)}, u32[]{:S(2)}) copy-start(f32[2,8,1024]{2,1,0:T(8,128)} %param.11) | copy-start | bytes 196612
  26.5 37.2 %copy-start.41 = (f32[1024]{0:T(1024)S(1)}, f32[1024]{0:T(1024)}, u32[]{:S(2)}) copy-start(f32[1024]{0:T(1024)} %param.13) | copy-start | bytes 12292
  26.6 38.5 %copy-start.40 = (f32[8,1024]{1,0:T(8,128)S(1)}, f32[8,1024]{1,0:T(8,128)}, u32[]{:S(2)}) copy-start(f32[8,1024]{1,0:T(8,128)} %param.12) | copy-start | bytes 98308
  28.5 37.2 %all-to-all-start = ((f32[2,16,8,256]{3,1,0,2:T(8,128)}), f32[2,16,8,256]{3,1,0,2:T(8,128)S(1)}, u32[]{:S(2)}, u32[]{:S(2)}) async-start(f32[2,16,8,256]{3,1,0,2:T(8,128)} %copy.120), calls=%async_computation | async-start | bytes 524288 | tf_op jit(solution)/shard_map/all_to_all | solution.py:31
  146.6 27.1 %copy-start.36 = (pred[2048]{0:T(1024)(128)(4,1)S(1)}, pred[2048]{0:T(1024)(128)(4,1)}, u32[]{:S(2)}) copy-start(pred[2048]{0:T(1024)(128)(4,1)} %copy-done.35) | copy-start | bytes 6148
  148.4 0.6 copy-start.11
  148.5 0.6 copy-start.13
  185.6 10.3 %all-to-all-start.1 = ((f32[2,16,8,256]{3,1,0,2:T(8,128)}), f32[2,16,8,256]{3,1,0,2:T(8,128)S(1)}, u32[]{:S(2)}, u32[]{:S(2)}) async-start(f32[2,16,8,256]{3,1,0,2:T(8,128)} %copy.139), calls=%async_computation.1 | async-start | bytes 524288 | tf_op jit(solution)/shard_map/all_to_all | solution.py:31
  261.4 10.4 %copy-start.9 = (f32[1024,2,16]{2,1,0:T(2,128)S(1)}, f32[1024,2,16]{2,1,0:T(2,128)}, u32[]{:S(2)}) copy-start(f32[1024,2,16]{2,1,0:T(2,128)} %gather_fusion.15) | copy-start | bytes 393220
  263.5 9.3 %copy-start.7 = (f32[1024,2,16]{2,1,0:T(2,128)S(1)}, f32[1024,2,16]{2,1,0:T(2,128)}, u32[]{:S(2)}) copy-start(f32[1024,2,16]{2,1,0:T(2,128)} %gather_fusion.16) | copy-start | bytes 393220
  265.6 7.6 %copy-start.5 = (f32[1024,2,16]{2,1,0:T(2,128)S(1)}, f32[1024,2,16]{2,1,0:T(2,128)}, u32[]{:S(2)}) copy-start(f32[1024,2,16]{2,1,0:T(2,128)} %gather_fusion.17) | copy-start | bytes 393220
  273.3 26.6 %copy-start.37 = (pred[2048]{0:T(1024)(128)(4,1)S(1)}, pred[2048]{0:T(1024)(128)(4,1)}, u32[]{:S(2)}) copy-start(pred[2048]{0:T(1024)(128)(4,1)} %copy-done.35) | copy-start | bytes 6148
  275.5 0.6 copy-start.15
  275.5 0.6 copy-start.17
  311.7 10.3 %all-to-all-start.2 = ((f32[2,16,8,256]{3,1,0,2:T(8,128)}), f32[2,16,8,256]{3,1,0,2:T(8,128)S(1)}, u32[]{:S(2)}, u32[]{:S(2)}) async-start(f32[2,16,8,256]{3,1,0,2:T(8,128)} %copy.158), calls=%async_computation.2 | async-start | bytes 524288 | tf_op jit(solution)/shard_map/all_to_all | solution.py:31
  387.6 10.4 %copy-start.10 = (f32[1024,2,16]{2,1,0:T(2,128)S(1)}, f32[1024,2,16]{2,1,0:T(2,128)}, u32[]{:S(2)}) copy-start(f32[1024,2,16]{2,1,0:T(2,128)} %gather_fusion.24) | copy-start | bytes 393220
  389.7 9.3 %copy-start.8 = (f32[1024,2,16]{2,1,0:T(2,128)S(1)}, f32[1024,2,16]{2,1,0:T(2,128)}, u32[]{:S(2)}) copy-start(f32[1024,2,16]{2,1,0:T(2,128)} %gather_fusion.25) | copy-start | bytes 393220
  391.8 7.6 %copy-start.6 = (f32[1024,2,16]{2,1,0:T(2,128)S(1)}, f32[1024,2,16]{2,1,0:T(2,128)}, u32[]{:S(2)}) copy-start(f32[1024,2,16]{2,1,0:T(2,128)} %gather_fusion.26) | copy-start | bytes 393220
  399.4 26.6 %copy-start.38 = (pred[2048]{0:T(1024)(128)(4,1)S(1)}, pred[2048]{0:T(1024)(128)(4,1)}, u32[]{:S(2)}) copy-start(pred[2048]{0:T(1024)(128)(4,1)} %copy-done.35) | copy-start | bytes 6148
  401.7 0.6 copy-start.19
  401.7 0.6 copy-start.21
  437.8 45.7 %copy-start.29 = (s32[1024]{0:T(1024)S(1)}, s32[1024]{0:T(1024)}, u32[]{:S(2)}) copy-start(s32[1024]{0:T(1024)} %fusion.113) | copy-start | bytes 12292
  437.8 10.4 %all-to-all-start.3 = ((f32[2,16,8,256]{3,1,0,2:T(8,128)}), f32[2,16,8,256]{3,1,0,2:T(8,128)S(1)}, u32[]{:S(2)}, u32[]{:S(2)}) async-start(f32[2,16,8,256]{3,1,0,2:T(8,128)} %copy.177), calls=%async_computation.3 | async-start | bytes 524288 | tf_op jit(solution)/shard_map/all_to_all | solution.py:31
  441.6 49.5 %copy-start.28 = (s32[1024]{0:T(1024)S(1)}, s32[1024]{0:T(1024)}, u32[]{:S(2)}) copy-start(s32[1024]{0:T(1024)} %fusion.114) | copy-start | bytes 12292
  513.6 6.2 %copy-start.1 = (f32[1024,2,16]{2,1,0:T(2,128)S(1)}, f32[1024,2,16]{2,1,0:T(2,128)}, u32[]{:S(2)}) copy-start(f32[1024,2,16]{2,1,0:T(2,128)} %gather_fusion.31) | copy-start | bytes 393220
  513.6 7.3 %copy-start.2 = (f32[1024,2,16]{2,1,0:T(2,128)S(1)}, f32[1024,2,16]{2,1,0:T(2,128)}, u32[]{:S(2)}) copy-start(f32[1024,2,16]{2,1,0:T(2,128)} %gather_fusion.32) | copy-start | bytes 393220
  513.6 8.4 %copy-start.3 = (f32[1024,2,16]{2,1,0:T(2,128)S(1)}, f32[1024,2,16]{2,1,0:T(2,128)}, u32[]{:S(2)}) copy-start(f32[1024,2,16]{2,1,0:T(2,128)} %gather_fusion.33) | copy-start | bytes 393220
  519.8 5.2 copy-start.30
  519.8 5.2 copy-start.31
  519.8 5.2 copy-start.32
  519.8 5.2 copy-start.33
  520.9 3.6 copy-start.4
  522.0 3.0 copy-start.20
  522.0 3.0 copy-start.22
  522.0 3.0 copy-start.23
  522.0 3.0 copy-start.24
  522.0 3.0 copy-start.25
  522.0 3.0 copy-start.26
  522.0 3.0 copy-start.27
  522.0 4.5 copy-start.12
  522.1 4.5 copy-start.14
  522.1 4.5 copy-start.16
  522.1 4.5 copy-start.18
